TPU v7x, 512 devices: a whole 4x8x8 slice. The times are simulated.
512 devices in a mesh: grow: 16 (over y, core), gcol: 32 (over x, z).
Axes of the slice: x: 4, y: 8, z: 8, core: 2. Of those that a mesh axis runs over, the one named last changes fastest.
Arguments:
- pair_density: bfloat16 [16384, 2048], P('gcol', 'grow'), may hold values from -0.125 to 0.125
- pair_weight: float32 [2048], P('grow'), may hold values from 0.25 to 4
- coulomb: float32 [16384], replicated, may hold values from 0.25 to 4
- pivot_rows: int32 [512], replicated, may hold values from 0 to 16383, as said below
Outputs:
- dielectric: float32 [16384, 16384], P('grow', 'gcol')
- panel_factor: float32 [16384, 512], P('grow')
Inputs may be any that keep to these rules, and one draw needn't show every extreme that they name: `pivot_rows`: 512 distinct plane-wave indices, exactly one in each run of 32 consecutive plane waves starting at a multiple of it; 0 and 16383 are always among them.
All inputs are finite; a program needn't handle non-finite values.
Results may differ from a plain program's by a relative error of at most 0.0038.
Values may be sent and summed in bfloat16 or wider, within the bound.
A program may use at most 64 MiB of HBM per device.

v0:
```python
import jax
import jax.numpy as jnp
from jax import lax
from jax.sharding import Mesh
from jax.sharding import PartitionSpec as P

NG = 16384
PANEL = 512
GCOL = ("gcol_0", "gcol_1")
GROW = ("grow_0", "grow_1")


def joined_along(blocks, dim):
    lengths = list(blocks.shape[1:])
    lengths[dim] *= blocks.shape[0]
    return jnp.moveaxis(blocks, 0, dim).reshape(lengths)


def gather_in_order(x, axes, sequence):
    blocks = x
    for k in sequence:
        blocks = lax.all_gather(blocks, axes[k])
    done = sequence[::-1]
    back = [done.index(k) for k in range(len(axes))]
    blocks = blocks.transpose(*back, *range(len(axes), blocks.ndim))
    return blocks.reshape(-1, *x.shape)


def gather_axes(x, axes, sequence, dim):
    return joined_along(gather_in_order(x, axes, sequence), dim)


def sent_to_all(x, axis):
    length = lax.axis_size(axis)
    return lax.all_to_all(jnp.broadcast_to(x[None], (length, *x.shape)), axis, 0, 0, tiled=True)


def collect(x, axis, dim):
    return joined_along(sent_to_all(x, axis), dim)


def padded_to(lines, length):
    spare = -len(lines) % length
    return jnp.pad(lines, [(0, spare)] + [(0, 0)] * (lines.ndim - 1))


def reduced_to_own(blocks, axes, sequence):
    lengths = [lax.axis_size(a) for a in axes]
    blocks = blocks.reshape(*lengths, *blocks.shape[1:])
    blocks = blocks.transpose(*sequence, *range(len(axes), blocks.ndim))
    blocks = blocks.reshape(-1, *blocks.shape[len(axes) :])
    for k in sequence:
        blocks = lax.psum_scatter(blocks, axes[k], scatter_dimension=0, tiled=True)
    return blocks[0]


def sum_by_parts(x, axes, sequence):
    length, lines = (lax.axis_size(axes), x.reshape(-1, *x.shape[1:][-1:]))
    blocks = padded_to(lines, length).reshape(length, -1, *lines.shape[1:])
    own = reduced_to_own(blocks, axes, sequence)
    whole = gather_in_order(own, axes, sequence[::-1]).reshape(-1, *lines.shape[1:])
    return whole[: len(lines)].reshape(x.shape)


def factor_rows(columns_in, row_numbers, pivot_block, pivot_rows):
    width = pivot_rows.shape[0]
    factor = jnp.linalg.cholesky(pivot_block)
    pivot_diag = jnp.diagonal(factor)
    solved = lax.linalg.triangular_solve(
        factor, columns_in, left_side=False, lower=True, transpose_a=True
    )
    lower_part = solved / pivot_diag[None, :]
    upper = pivot_diag[:, None] * factor.T
    column_iota = lax.iota(jnp.int32, width)
    matches = row_numbers[:, None] == pivot_rows[None, :]
    is_pivot = jnp.any(matches, axis=1)
    position = jnp.sum(jnp.where(matches, column_iota[None, :], 0), axis=1)
    top_rows = jnp.take(upper, position, axis=0)
    upper_mask = is_pivot[:, None] & (column_iota[None, :] >= position[:, None])
    return jnp.where(upper_mask, top_rows, lower_part)


def select_rows(columns_in, first_row, pivot_rows):
    count_rows = columns_in.shape[0]
    offsets = pivot_rows - first_row
    inside = (offsets >= 0) & (offsets < count_rows)
    taken = jnp.take(columns_in, jnp.clip(offsets, 0, count_rows - 1), axis=0)
    return jnp.where(inside[:, None], taken, 0.0)


def body(pair_density, pair_weight, coulomb, pivot_rows):
    col_ratio = lax.axis_size(GCOL) // lax.axis_size(GROW)
    row_id = lax.axis_index(GROW)
    col_id = lax.axis_index(GCOL)
    scaled = (pair_density.astype(jnp.float32) * jnp.sqrt(pair_weight)[None, :]).astype(
        jnp.bfloat16
    )
    width_cols = scaled.shape[0]
    width_rows = width_cols * col_ratio
    contract = (((1,), (1,)), ((), ()))
    every_wave = gather_axes(scaled, GCOL, (0, 1), 0)
    row_side = lax.all_to_all(every_wave, GROW, split_axis=0, concat_axis=1, tiled=True)
    gram_block = lax.dot_general(
        row_side, collect(scaled, GROW, 1), contract, preferred_element_type=jnp.float32
    )
    first_global = row_id * width_rows
    row_numbers = first_global + lax.iota(jnp.int32, width_rows)
    col_numbers = col_id * width_cols + lax.iota(jnp.int32, width_cols)
    row_scale = jnp.sqrt(lax.dynamic_slice_in_dim(coulomb, first_global, width_rows))
    col_scale = jnp.sqrt(lax.dynamic_slice_in_dim(coulomb, col_id * width_cols, width_cols))
    identity = jnp.where(row_numbers[:, None] == col_numbers[None, :], 1.0, 0.0).astype(jnp.float32)
    dielectric = row_scale[:, None] * col_scale[None, :] * gram_block + identity
    stride = NG // PANEL
    per_device = width_cols // stride
    run_of = pivot_rows // stride
    run_pivot = jnp.zeros((PANEL,), jnp.int32).at[run_of].set(pivot_rows)
    local_cols = (
        lax.dynamic_slice_in_dim(run_pivot, col_id * per_device, per_device) - col_id * width_cols
    )
    own_columns = jnp.take(dielectric, local_cols, axis=1)
    run_columns = lax.all_gather(own_columns, GCOL, axis=1, tiled=True)
    columns = jnp.take(run_columns, run_of, axis=1)
    pivot_block = sum_by_parts(select_rows(columns, first_global, pivot_rows), GROW, (0, 1))
    panel_out = factor_rows(columns, row_numbers, pivot_block, pivot_rows)
    return (dielectric, panel_out)


def solution(mesh):
    finer = Mesh(mesh.devices.reshape(8, 2, 4, 8), ("grow_0", "grow_1", "gcol_0", "gcol_1"))
    return jax.shard_map(
        body,
        mesh=finer,
        in_specs=(P(GCOL, GROW), P(GROW), P(), P()),
        out_specs=(P(GROW, GCOL), P(GROW, None)),
        check_vma=False,
    )
```

profile of v0, /device:TPU:2, one launch (start us, length us, event | category | flops | bytes accessed | tf_op | source)
XLA Modules:
  0.0 581.8 jit_solution(7937591395494677095)
XLA Ops:
  8.8 16.2 %all-gather = bf16[2048,128]{1,0:T(8,128)(2,1)} all-gather(bf16[512,128]{1,0:T(8,128)(2,1)S(1)} %multiply_convert_fusion), channel_id=2, replica_groups=mesh['grow_0'=8,'grow_1'=2,'gcol_0'=4,'gcol_1'=8] {'gcol_0'}, dimensions={0}, use_global_device_ids=true | all-gather | bytes 655360 | tf_op jit(solution)/shard_map/all_gather | solution.py:22
  26.7 5.3 all-to-all-start.1
  32.0 53.7 %all-gather.9.cloned.1.call-done = bf16[32,512,128]{2,1,0:T(8,128)(2,1)} async-done(((bf16[4,512,128]{2,1,0:T(8,128)(2,1)}), bf16[32,512,128]{2,1,0:T(8,128)(2,1)}) %all-gather.9.cloned.1.call-update) | async-done | bytes 4194320 | tf_op jit(solution)/shard_map/all_gather | solution.py:22
  85.8 4.6 copy.20
  90.3 7.0 %all-to-all-start = ((bf16[16,1024,128]{2,1,0:T(8,128)(2,1)}), bf16[16,1024,128]{2,1,0:T(8,128)(2,1)}, u32[]{:S(2)}, u32[]{:S(2)}) async-start(bf16[16,1024,128]{2,1,0:T(8,128)(2,1)} %bitcast.81), calls=%async_computation | async-start | bytes 8388608 | tf_op jit(solution)/shard_map/all_to_all | solution.py:102
  101.5 90.2 %all-to-all-done = bf16[16,1024,128]{2,1,0:T(8,128)(2,1)} async-done(((bf16[16,1024,128]{2,1,0:T(8,128)(2,1)}), bf16[16,1024,128]{2,1,0:T(8,128)(2,1)}, u32[]{:S(2)}, u32[]{:S(2)}) %all-to-all-start) | async-done | bytes 4194336 | tf_op jit(solution)/shard_map/all_to_all | solution.py:102
  191.7 5.9 %fusion.4 = f32[1024,512]{1,0:T(8,128)} fusion(bf16[16,512,128]{2,1,0:T(8,128)(2,1)S(1)} %all-to-all-done.1, bf16[16,1024,128]{2,1,0:T(8,128)(2,1)} %all-to-all-done, s32[512]{0:T(512)S(1)} %iota_add_fusion.1, f32[512]{0:T(512)S(1)} %dynamic-slice_sqrt_fusion.1, f32[1024]{0:T(1024)S(1)} %dynamic-slice_sqrt_fusion, s32[1024]{0:T(1024)S(1)} %iota_add_fusion), kind=kOutput, calls=%fused_computation.16 | convolution fusion | flops 2150105088 | bytes 8400896 | tf_op jit(solution)/shard_map/dot_general | solution.py:103
  201.1 78.4 %all-gather.7.cloned.1.call-done = f32[1024,512]{0,1:T(8,128)} async-done(((f32[1024,16]{0,1:T(8,128)}), f32[1024,512]{0,1:T(8,128)}) %all-gather.7.cloned.1.call-update) | async-done | bytes 2097168 | tf_op jit(solution)/shard_map/all_gather | solution.py:121
  279.5 4.4 gather_fusion.1
  290.4 39.5 %reduce-scatter.3.cloned.1.call-done = f32[2,32,512]{2,1,0:T(8,128)} async-done(((f32[16,32,512]{2,1,0:T(8,128)}), f32[2,32,512]{2,1,0:T(8,128)}) %reduce-scatter.3.cloned.1.call-update) | async-done | bytes 131088 | tf_op jit(solution)/shard_map/reduce_scatter | solution.py:53
  330.0 17.3 %reduce-scatter.5.cloned.1.call-done = f32[1,32,512]{2,1,0:T(8,128)} async-done(((f32[2,32,512]{2,1,0:T(8,128)}), f32[1,32,512]{2,1,0:T(8,128)}) %reduce-scatter.5.cloned.1.call-update) | async-done | bytes 65552 | tf_op jit(solution)/shard_map/reduce_scatter | solution.py:53
  347.3 4.0 all_gather.29
  352.3 41.3 %all-gather.11.cloned.1.call-done = f32[16,32,512]{2,1,0:T(8,128)} async-done(((f32[2,32,512]{2,1,0:T(8,128)}), f32[16,32,512]{2,1,0:T(8,128)}) %all-gather.11.cloned.1.call-update) | async-done | bytes 1048592 | tf_op jit(solution)/shard_map/all_gather | solution.py:22
  398.6 11.7 %cholesky.102 = f32[128,128]{1,0:T(8,128)S(1)} custom-call(f32[128,128]{1,0:T(8,128)S(1)} %cholesky.260), custom_call_target="Cholesky" | custom-call | tf_op jit(solution)/shard_map/jit(cholesky)/cholesky | solution.py:67
  410.3 9.8 %custom-call.30 = f32[1,128,128]{1,2,0:T(8,128)S(1)} custom-call(f32[1,128,128]{2,1,0:T(8,128)S(1)} %get-tuple-element.43), custom_call_target="InvertDiagBlocksLowerTriangular" | custom-call | tf_op jit(solution)/shard_map/jit(cholesky)/cholesky | solution.py:67
  422.8 11.7 %cholesky.213 = f32[128,128]{1,0:T(8,128)S(1)} custom-call(f32[128,128]{1,0:T(8,128)S(1)} %cholesky.264), custom_call_target="Cholesky" | custom-call | tf_op jit(solution)/shard_map/jit(cholesky)/cholesky | solution.py:67
  434.6 9.9 %custom-call.31 = f32[1,128,128]{1,2,0:T(8,128)S(1)} custom-call(f32[1,128,128]{2,1,0:T(8,128)S(1)} %get-tuple-element.40), custom_call_target="InvertDiagBlocksLowerTriangular" | custom-call | tf_op jit(solution)/shard_map/jit(cholesky)/cholesky | solution.py:67
  446.1 11.7 %cholesky.234 = f32[128,128]{1,0:T(8,128)S(1)} custom-call(f32[128,128]{1,0:T(8,128)S(1)} %cholesky.269), custom_call_target="Cholesky" | custom-call | tf_op jit(solution)/shard_map/jit(cholesky)/cholesky | solution.py:67
  458.5 9.8 %custom-call.32 = f32[1,128,128]{1,2,0:T(8,128)S(1)} custom-call(f32[1,128,128]{2,1,0:T(8,128)S(1)} %get-tuple-element.37), custom_call_target="InvertDiagBlocksLowerTriangular" | custom-call | tf_op jit(solution)/shard_map/jit(cholesky)/cholesky | solution.py:67
  469.8 11.9 %cholesky.251 = f32[128,128]{1,0:T(8,128)S(1)} custom-call(f32[128,128]{1,0:T(8,128)S(1)} %convolution_subtract_fusion.4), custom_call_target="Cholesky" | custom-call | tf_op jit(solution)/shard_map/jit(cholesky)/cholesky | solution.py:67
  488.0 4.5 gather_fusion.3
  495.2 14.0 %while.1 = (s32[]{:T(128)}, f32[512,512]{1,0:T(8,128)}, s32[4,2]{0,1:T(2,128)S(1)}, f32[4,128,128]{2,1,0:T(8,128)}, s32[]{:T(128)}) while((s32[]{:T(128)}, f32[512,512]{1,0:T(8,128)}, s32[4,2]{0,1:T(2,128)S(1)}, f32[4,128,128]{2,1,0:T(8,128)}, s32[]{:T(128)}) %tuple.42), condition=%wide.while_cond, body=%wide.while_body.sunk | while | flops 2 | bytes 132205 | solution.py:69
  495.9 2.9 bitcast_dynamic-update-slice_fusion.2
  499.4 2.9 bitcast_dynamic-update-slice_fusion.2
  502.9 2.9 bitcast_dynamic-update-slice_fusion.2
  509.2 40.1 %custom-call.33 = f32[4,128,128]{1,2,0:T(8,128)S(1)} custom-call(f32[4,128,128]{2,1,0:T(8,128)} %get-tuple-element.9), custom_call_target="InvertDiagBlocksLowerTriangular" | custom-call | tf_op jit(solution)/shard_map/triangular_solve | solution.py:69
  552.5 2.9 convolution_subtract_fusion
  556.0 3.8 fusion.17
  560.5 4.9 gather_fusion.4
  565.4 3.0 copy.25
  568.4 3.7 fusion.3
  572.1 2.9 copy.26
  (98 shorter events, 46.0 us)
Async XLA Ops:
  7.2 78.6 %all-gather.9.cloned.1.call-start = ((), (), s32[]{:S(2)}) async-start(), calls=%async_computation.7 | async-start | bytes 4718592 | tf_op jit(solution)/shard_map/all_gather | solution.py:22
  26.7 63.6 %all-to-all-start.1 = ((bf16[16,512,128]{2,1,0:T(8,128)(2,1)}), bf16[16,512,128]{2,1,0:T(8,128)(2,1)S(1)}, u32[]{:S(2)}, u32[]{:S(2)}) async-start(bf16[16,512,128]{2,1,0:T(8,128)(2,1)} %broadcast_in_dim.109), calls=%async_computation.1 | async-start | bytes 4194304 | tf_op jit(solution)/shard_map/all_to_all | solution.py:35
  90.3 7.1 %copy-start.9 = (s32[512]{0:T(512)S(1)}, s32[512]{0:T(512)}, u32[]{:S(2)}) copy-start(s32[512]{0:T(512)} %param.7) | copy-start | bytes 6148
  90.3 101.4 %all-to-all-start = ((bf16[16,1024,128]{2,1,0:T(8,128)(2,1)}), bf16[16,1024,128]{2,1,0:T(8,128)(2,1)}, u32[]{:S(2)}, u32[]{:S(2)}) async-start(bf16[16,1024,128]{2,1,0:T(8,128)(2,1)} %bitcast.81), calls=%async_computation | async-start | bytes 8388608 | tf_op jit(solution)/shard_map/all_to_all | solution.py:102
  97.4 182.1 %all-gather.7.cloned.1.call-start = ((), (), s32[]{:S(2)}) async-start(), calls=%async_computation.4 | async-start | bytes 2162688 | tf_op jit(solution)/shard_map/all_gather | solution.py:121
  200.9 129.1 %reduce-scatter.3.cloned.1.call-start = ((), (), s32[]{:S(2)}) async-start(), calls=%async_computation.5 | async-start | bytes 1179648 | tf_op jit(solution)/shard_map/reduce_scatter | solution.py:53
  290.4 57.0 %reduce-scatter.5.cloned.1.call-start = ((), (), s32[]{:S(2)}) async-start(), calls=%async_computation.6 | async-start | bytes 196608 | tf_op jit(solution)/shard_map/reduce_scatter | solution.py:53
  330.0 63.6 %all-gather.11.cloned.1.call-start = ((), (), s32[]{:S(2)}) async-start(), calls=%async_computation.8 | async-start | bytes 1179648 | tf_op jit(solution)/shard_map/all_gather | solution.py:22
  393.6 2.6 copy-start.7
  397.6 1.0 copy-start.8
  481.7 3.9 copy-start.4
  550.0 6.1 %copy-start = (f32[1024,128]{0,1:T(8,128)}, f32[1024,128]{0,1:T(8,128)S(1)}, u32[]{:S(2)}) copy-start(f32[1024,128]{0,1:T(8,128)S(1)} %fusion.25) | copy-start | bytes 1572868
  552.5 7.3 %copy-start.2 = (f32[1024,128]{0,1:T(8,128)}, f32[1024,128]{0,1:T(8,128)S(1)}, u32[]{:S(2)}) copy-start(f32[1024,128]{0,1:T(8,128)S(1)} %fusion.37) | copy-start | bytes 1572868
  556.0 3.8 copy-start.5
  565.4 3.1 copy-start.1
  565.4 3.1 copy-start.3
  565.4 3.1 copy-start.6
Sparse Core Ops, SparseCore 0:
  25.1 60.5 all-gather.8
  201.0 78.4 all-gather.6
  290.5 39.4 reduce-scatter.2
  332.6 14.7 reduce-scatter.4
  351.5 42.0 all-gather.10
where the time goes:
time: 588 us; the launch traced here: 582 us
  waiting for transfers between devices  321 us (55%)
  other arithmetic  133 us (23%)
  local copies, waits for them, and re-layouts  56 us (10%)
  matrix products  22.4 us (4%)
  blocking collectives  20.2 us (3%)
  between operations  16.8 us (3%)
  starting transfers between devices  12.5 us (2%)
    all_gather x2, waiting for transfers between devices, gather_in_order(): blocks = lax.all_gather(blocks, axes[k])  95 us
    all_to_all x1, waiting for transfers between devices, body(): lax.all_to_all(every_wave, GROW, split_axis=0, concat_axis=1, tiled=True)  90.2 us
    another operation x14, other arithmetic, factor_rows(): factor = jnp.linalg.cholesky(pivot_block)  78.9 us
    all_gather x1, waiting for transfers between devices, body(): run_columns = lax.all_gather(own_columns, GCOL, axis=1, tiled=True)  78.4 us
    reduce_scatter x2, waiting for transfers between devices, reduced_to_own(): blocks = lax.psum_scatter(blocks, axes[k], scatter_dimension=0, tiled=True)  56.8 us
    another operation x3, other arithmetic, factor_rows(): lax.linalg.triangular_solve(factor, columns_in, left_side=False, lower=Tr...  42.5 us
    all_gather x2, blocking collectives, gather_in_order(): blocks = lax.all_gather(blocks, axes[k])  20.2 us
    another operation x12, local copies, waits for them, and re-layouts  14 us
  transfers between devices with their start and end apart: 7, of which 6 were waited for; matrix products, arithmetic and copies ran while one was open for 2% of the time, Pallas kernels for 0%

commit v1 on v0

--- a/solution.py
+++ b/solution.py
@@ -118,7 +118,9 @@
         lax.dynamic_slice_in_dim(run_pivot, col_id * per_device, per_device) - col_id * width_cols
     )
     own_columns = jnp.take(dielectric, local_cols, axis=1)
-    run_columns = lax.all_gather(own_columns, GCOL, axis=1, tiled=True)
+    run_columns = jnp.concatenate(
+        lax.all_to_all(jnp.stack([own_columns] * lax.axis_size(GCOL)), GCOL, 0, 0), axis=1
+    )
     columns = jnp.take(run_columns, run_of, axis=1)
     pivot_block = sum_by_parts(select_rows(columns, first_global, pivot_rows), GROW, (0, 1))
     panel_out = factor_rows(columns, row_numbers, pivot_block, pivot_rows)

time: 588 us -> 565 us (0.961)
  waiting for transfers between devices: 321 us -> 289 us
  starting transfers between devices: 12.5 us -> 19.7 us
    all_gather x1 -> x0, waiting for transfers between devices: 78.4 us -> none  [body(): run_columns = lax.all_gather(own_columns, GCOL, axis=1, tiled=True)]
    all_to_all x0 -> x1, waiting for transfers between devices: none -> 46.9 us  [body(): lax.all_to_all(jnp.stack([own_columns] * lax.axis_size(GCOL)), GCOL, 0, 0)]
    all_to_all x0 -> x1, starting transfers between devices: none -> 7.27 us  [body(): lax.all_to_all(jnp.stack([own_columns] * lax.axis_size(GCOL)), GCOL, 0, 0)]
    another operation x12 -> x13, local copies, waits for them, and re-layouts: 14 us -> 15.7 us
where the time goes in v1:
time: 565 us; the launch traced here: 558 us
  waiting for transfers between devices  289 us (51%)
  other arithmetic  133 us (24%)
  local copies, waits for them, and re-layouts  57 us (10%)
  matrix products  22.4 us (4%)
  blocking collectives  20.2 us (4%)
  starting transfers between devices  19.7 us (3%)
  between operations  16.9 us (3%)
    all_gather x2, waiting for transfers between devices, gather_in_order(): blocks = lax.all_gather(blocks, axes[k])  95 us
    all_to_all x1, waiting for transfers between devices, body(): lax.all_to_all(every_wave, GROW, split_axis=0, concat_axis=1, tiled=True)  90.3 us
    another operation x14, other arithmetic, factor_rows(): factor = jnp.linalg.cholesky(pivot_block)  78.9 us
    reduce_scatter x2, waiting for transfers between devices, reduced_to_own(): blocks = lax.psum_scatter(blocks, axes[k], scatter_dimension=0, tiled=True)  56.7 us
    all_to_all x1, waiting for transfers between devices, body(): lax.all_to_all(jnp.stack([own_columns] * lax.axis_size(GCOL)), GCOL, 0, 0)  46.9 us
    another operation x3, other arithmetic, factor_rows(): lax.linalg.triangular_solve(factor, columns_in, left_side=False, lower=Tr...  42.5 us
    all_gather x2, blocking collectives, gather_in_order(): blocks = lax.all_gather(blocks, axes[k])  20.2 us
    another operation x12, local copies, waits for them, and re-layouts  14.1 us
  transfers between devices with their start and end apart: 7, of which 6 were waited for; matrix products, arithmetic and copies ran while one was open for 2% of the time, Pallas kernels for 0%

profile of v1, /device:TPU:2, one launch (start us, length us, event | category | flops | bytes accessed | tf_op | source)
XLA Modules:
  0.0 557.9 jit_solution(3179390964051111690)
XLA Ops:
  8.8 16.2 %all-gather = bf16[2048,128]{1,0:T(8,128)(2,1)} all-gather(bf16[512,128]{1,0:T(8,128)(2,1)S(1)} %multiply_convert_fusion), channel_id=2, replica_groups=mesh['grow_0'=8,'grow_1'=2,'gcol_0'=4,'gcol_1'=8] {'gcol_0'}, dimensions={0}, use_global_device_ids=true | all-gather | bytes 655360 | tf_op jit(solution)/shard_map/all_gather | solution.py:22
  26.7 5.3 all-to-all-start.1
  32.0 53.7 %all-gather.6.cloned.1.call-done = bf16[32,512,128]{2,1,0:T(8,128)(2,1)} async-done(((bf16[4,512,128]{2,1,0:T(8,128)(2,1)}), bf16[32,512,128]{2,1,0:T(8,128)(2,1)}) %all-gather.6.cloned.1.call-update) | async-done | bytes 4194320 | tf_op jit(solution)/shard_map/all_gather | solution.py:22
  85.8 4.6 copy.20
  90.3 7.0 %all-to-all-start = ((bf16[16,1024,128]{2,1,0:T(8,128)(2,1)}), bf16[16,1024,128]{2,1,0:T(8,128)(2,1)}, u32[]{:S(2)}, u32[]{:S(2)}) async-start(bf16[16,1024,128]{2,1,0:T(8,128)(2,1)} %bitcast.85), calls=%async_computation | async-start | bytes 8388608 | tf_op jit(solution)/shard_map/all_to_all | solution.py:102
  101.4 90.3 %all-to-all-done = bf16[16,1024,128]{2,1,0:T(8,128)(2,1)} async-done(((bf16[16,1024,128]{2,1,0:T(8,128)(2,1)}), bf16[16,1024,128]{2,1,0:T(8,128)(2,1)}, u32[]{:S(2)}, u32[]{:S(2)}) %all-to-all-start) | async-done | bytes 4194336 | tf_op jit(solution)/shard_map/all_to_all | solution.py:102
  191.7 5.9 %fusion.4 = f32[1024,512]{1,0:T(8,128)} fusion(bf16[16,512,128]{2,1,0:T(8,128)(2,1)S(1)} %all-to-all-done.1, bf16[16,1024,128]{2,1,0:T(8,128)(2,1)} %all-to-all-done, s32[512]{0:T(512)S(1)} %iota_add_fusion.1, f32[512]{0:T(512)S(1)} %dynamic-slice_sqrt_fusion.1, f32[1024]{0:T(1024)S(1)} %dynamic-slice_sqrt_fusion, s32[1024]{0:T(1024)S(1)} %iota_add_fusion), kind=kOutput, calls=%fused_computation.16 | convolution fusion | flops 2150105088 | bytes 8400896 | tf_op jit(solution)/shard_map/dot_general | solution.py:103
  201.8 7.3 %all-to-all-start.2 = ((f32[32,1024,16]{1,2,0:T(8,128)}), f32[32,1024,16]{1,2,0:T(8,128)S(1)}, u32[]{:S(2)}, u32[]{:S(2)}) async-start(f32[32,1024,16]{1,2,0:T(8,128)} %stack.2), calls=%async_computation.2 | async-start | bytes 4194304 | tf_op jit(solution)/shard_map/all_to_all | solution.py:122
  209.3 46.9 %all-to-all-done.2 = f32[32,1024,16]{1,2,0:T(8,128)S(1)} async-done(((f32[32,1024,16]{1,2,0:T(8,128)}), f32[32,1024,16]{1,2,0:T(8,128)S(1)}, u32[]{:S(2)}, u32[]{:S(2)}) %all-to-all-start.2) | async-done | bytes 2097184 | tf_op jit(solution)/shard_map/all_to_all | solution.py:122
  258.9 2.9 copy.22
  266.5 39.3 %reduce-scatter.3.cloned.1.call-done = f32[2,32,512]{2,1,0:T(8,128)} async-done(((f32[16,32,512]{2,1,0:T(8,128)}), f32[2,32,512]{2,1,0:T(8,128)}) %reduce-scatter.3.cloned.1.call-update) | async-done | bytes 131088 | tf_op jit(solution)/shard_map/reduce_scatter | solution.py:53
  305.9 17.5 %reduce-scatter.5.cloned.1.call-done = f32[1,32,512]{2,1,0:T(8,128)} async-done(((f32[2,32,512]{2,1,0:T(8,128)}), f32[1,32,512]{2,1,0:T(8,128)}) %reduce-scatter.5.cloned.1.call-update) | async-done | bytes 65552 | tf_op jit(solution)/shard_map/reduce_scatter | solution.py:53
  323.4 4.0 all_gather.25
  328.3 41.3 %all-gather.8.cloned.1.call-done = f32[16,32,512]{2,1,0:T(8,128)} async-done(((f32[2,32,512]{2,1,0:T(8,128)}), f32[16,32,512]{2,1,0:T(8,128)}) %all-gather.8.cloned.1.call-update) | async-done | bytes 1048592 | tf_op jit(solution)/shard_map/all_gather | solution.py:22
  374.6 11.7 %cholesky.102 = f32[128,128]{1,0:T(8,128)S(1)} custom-call(f32[128,128]{1,0:T(8,128)S(1)} %cholesky.260), custom_call_target="Cholesky" | custom-call | tf_op jit(solution)/shard_map/jit(cholesky)/cholesky | solution.py:67
  386.3 9.8 %custom-call.30 = f32[1,128,128]{1,2,0:T(8,128)S(1)} custom-call(f32[1,128,128]{2,1,0:T(8,128)S(1)} %get-tuple-element.43), custom_call_target="InvertDiagBlocksLowerTriangular" | custom-call | tf_op jit(solution)/shard_map/jit(cholesky)/cholesky | solution.py:67
  398.8 11.7 %cholesky.213 = f32[128,128]{1,0:T(8,128)S(1)} custom-call(f32[128,128]{1,0:T(8,128)S(1)} %cholesky.264), custom_call_target="Cholesky" | custom-call | tf_op jit(solution)/shard_map/jit(cholesky)/cholesky | solution.py:67
  410.6 9.9 %custom-call.31 = f32[1,128,128]{1,2,0:T(8,128)S(1)} custom-call(f32[1,128,128]{2,1,0:T(8,128)S(1)} %get-tuple-element.40), custom_call_target="InvertDiagBlocksLowerTriangular" | custom-call | tf_op jit(solution)/shard_map/jit(cholesky)/cholesky | solution.py:67
  422.1 11.7 %cholesky.234 = f32[128,128]{1,0:T(8,128)S(1)} custom-call(f32[128,128]{1,0:T(8,128)S(1)} %cholesky.269), custom_call_target="Cholesky" | custom-call | tf_op jit(solution)/shard_map/jit(cholesky)/cholesky | solution.py:67
  434.5 9.8 %custom-call.32 = f32[1,128,128]{1,2,0:T(8,128)S(1)} custom-call(f32[1,128,128]{2,1,0:T(8,128)S(1)} %get-tuple-element.37), custom_call_target="InvertDiagBlocksLowerTriangular" | custom-call | tf_op jit(solution)/shard_map/jit(cholesky)/cholesky | solution.py:67
  445.8 11.9 %cholesky.251 = f32[128,128]{1,0:T(8,128)S(1)} custom-call(f32[128,128]{1,0:T(8,128)S(1)} %convolution_subtract_fusion.4), custom_call_target="Cholesky" | custom-call | tf_op jit(solution)/shard_map/jit(cholesky)/cholesky | solution.py:67
  464.0 4.5 gather_fusion.3
  471.2 14.1 %while.1 = (s32[]{:T(128)}, f32[512,512]{1,0:T(8,128)}, s32[4,2]{0,1:T(2,128)S(1)}, f32[4,128,128]{2,1,0:T(8,128)}, s32[]{:T(128)}) while((s32[]{:T(128)}, f32[512,512]{1,0:T(8,128)}, s32[4,2]{0,1:T(2,128)S(1)}, f32[4,128,128]{2,1,0:T(8,128)}, s32[]{:T(128)}) %tuple.42), condition=%wide.while_cond, body=%wide.while_body.sunk | while | flops 2 | bytes 132205 | solution.py:69
  471.9 2.9 bitcast_dynamic-update-slice_fusion.2
  475.4 2.9 bitcast_dynamic-update-slice_fusion.2
  479.0 2.9 bitcast_dynamic-update-slice_fusion.2
  485.4 40.1 %custom-call.33 = f32[4,128,128]{1,2,0:T(8,128)S(1)} custom-call(f32[4,128,128]{2,1,0:T(8,128)} %get-tuple-element.9), custom_call_target="InvertDiagBlocksLowerTriangular" | custom-call | tf_op jit(solution)/shard_map/triangular_solve | solution.py:69
  532.2 3.8 fusion.17
  536.6 4.9 gather_fusion.4
  541.5 3.1 copy.25
  544.6 3.7 fusion.3
  548.3 2.9 copy.26
  (98 shorter events, 50.6 us)
Async XLA Ops:
  7.2 78.6 %all-gather.6.cloned.1.call-start = ((), (), s32[]{:S(2)}) async-start(), calls=%async_computation.7 | async-start | bytes 4718592 | tf_op jit(solution)/shard_map/all_gather | solution.py:22
  26.7 63.6 %all-to-all-start.1 = ((bf16[16,512,128]{2,1,0:T(8,128)(2,1)}), bf16[16,512,128]{2,1,0:T(8,128)(2,1)S(1)}, u32[]{:S(2)}, u32[]{:S(2)}) async-start(bf16[16,512,128]{2,1,0:T(8,128)(2,1)} %broadcast_in_dim.109), calls=%async_computation.1 | async-start | bytes 4194304 | tf_op jit(solution)/shard_map/all_to_all | solution.py:35
  90.3 7.0 %copy-start.9 = (s32[512]{0:T(512)S(1)}, s32[512]{0:T(512)}, u32[]{:S(2)}) copy-start(s32[512]{0:T(512)} %param.7) | copy-start | bytes 6148
  90.3 101.4 %all-to-all-start = ((bf16[16,1024,128]{2,1,0:T(8,128)(2,1)}), bf16[16,1024,128]{2,1,0:T(8,128)(2,1)}, u32[]{:S(2)}, u32[]{:S(2)}) async-start(bf16[16,1024,128]{2,1,0:T(8,128)(2,1)} %bitcast.85), calls=%async_computation | async-start | bytes 8388608 | tf_op jit(solution)/shard_map/all_to_all | solution.py:102
  201.8 54.5 %all-to-all-start.2 = ((f32[32,1024,16]{1,2,0:T(8,128)}), f32[32,1024,16]{1,2,0:T(8,128)S(1)}, u32[]{:S(2)}, u32[]{:S(2)}) async-start(f32[32,1024,16]{1,2,0:T(8,128)} %stack.2), calls=%async_computation.2 | async-start | bytes 4194304 | tf_op jit(solution)/shard_map/all_to_all | solution.py:122
  209.1 96.7 %reduce-scatter.3.cloned.1.call-start = ((), (), s32[]{:S(2)}) async-start(), calls=%async_computation.5 | async-start | bytes 1179648 | tf_op jit(solution)/shard_map/reduce_scatter | solution.py:53
  266.5 56.9 %reduce-scatter.5.cloned.1.call-start = ((), (), s32[]{:S(2)}) async-start(), calls=%async_computation.6 | async-start | bytes 196608 | tf_op jit(solution)/shard_map/reduce_scatter | solution.py:53
  305.8 63.8 %all-gather.8.cloned.1.call-start = ((), (), s32[]{:S(2)}) async-start(), calls=%async_computation.8 | async-start | bytes 1179648 | tf_op jit(solution)/shard_map/all_gather | solution.py:22
  369.6 2.6 copy-start.7
  373.6 1.0 copy-start.8
  457.7 4.0 copy-start.4
  526.1 6.1 %copy-start = (f32[1024,128]{0,1:T(8,128)}, f32[1024,128]{0,1:T(8,128)S(1)}, u32[]{:S(2)}) copy-start(f32[1024,128]{0,1:T(8,128)S(1)} %fusion.25) | copy-start | bytes 1572868
  528.7 7.3 %copy-start.2 = (f32[1024,128]{0,1:T(8,128)}, f32[1024,128]{0,1:T(8,128)S(1)}, u32[]{:S(2)}) copy-start(f32[1024,128]{0,1:T(8,128)S(1)} %fusion.37) | copy-start | bytes 1572868
  532.2 3.8 copy-start.5
  541.5 3.1 copy-start.1
  541.5 3.1 copy-start.3
  541.5 3.1 copy-start.6
Sparse Core Ops, SparseCore 0:
  25.1 60.5 all-gather.5
  266.6 39.1 reduce-scatter.2
  308.6 14.7 reduce-scatter.4
  327.5 42.0 all-gather.7
